TPU v7x, 32 devices: a whole 2x2x4 slice. The times are simulated.
32 devices in a mesh: dp: 4 (over z), blk: 2 (over x), ulys: 4 (over y, core).
Axes of the slice: x: 2, y: 2, z: 4, core: 2. Of those that a mesh axis runs over, the one named last changes fastest.
Arguments:
- hidden: float32 [6144, 768], P(('dp', 'blk', 'ulys')), may hold values from -6 to 6
- time_embed: float32 [4, 768], P('dp'), may hold values from -6 to 6
- segment_ids: int32 [4, 1536], P('dp', 'blk'), may hold values from 0 to 7, never falling along the last dimension, each value on 1 to 384 neighbouring positions
- key_valid: int32 [4, 1536], P('dp', 'blk'), may hold values 0 or 1
- out_grad: float32 [6144, 768], P(('dp', 'blk', 'ulys')), may hold values from -6 to 6
- w_query: float32 [768, 768], P(('blk', 'ulys')), may hold values from -0.21875 to 0.21875
- b_query: float32 [768], P(('blk', 'ulys')), may hold values from -3 to 3
- w_key: float32 [768, 768], P(('blk', 'ulys')), may hold values from -0.21875 to 0.21875
- w_value: float32 [768, 768], P(('blk', 'ulys')), may hold values from -0.21875 to 0.21875
- b_value: float32 [768], P(('blk', 'ulys')), may hold values from -3 to 3
- w_out: float32 [768, 768], P(('blk', 'ulys')), may hold values from -3 to 3
- b_out: float32 [768], P(('blk', 'ulys')), may hold values from -3 to 3
- w_up: float32 [768, 3072], P(('blk', 'ulys')), may hold values from -0.21875 to 0.21875
- b_up: float32 [3072], P(('blk', 'ulys')), may hold values from -3 to 3
- w_down: float32 [3072, 768], P(('blk', 'ulys')), may hold values from -0.109375 to 0.109375
- b_down: float32 [768], P(('blk', 'ulys')), may hold values from -3 to 3
- pre_gain: float32 [768], P(('blk', 'ulys')), may hold values from 0.5 to 1.5
- pre_shift: float32 [768], P(('blk', 'ulys')), may hold values from -3 to 3
- mlp_gain: float32 [768], P(('blk', 'ulys')), may hold values from 0.5 to 1.5
- mlp_shift: float32 [768], P(('blk', 'ulys')), may hold values from -3 to 3
Outputs:
- output: float32 [6144, 768], P(('dp', 'blk', 'ulys'))
- hidden_grad: float32 [6144, 768], P(('dp', 'blk', 'ulys'))
- grad_query: float32 [768, 768], P(('blk', 'ulys'))
- grad_qbias: float32 [768], P(('blk', 'ulys'))
- grad_key: float32 [768, 768], P(('blk', 'ulys'))
- grad_value: float32 [768, 768], P(('blk', 'ulys'))
- grad_vbias: float32 [768], P(('blk', 'ulys'))
- grad_outproj: float32 [768, 768], P(('blk', 'ulys'))
- grad_obias: float32 [768], P(('blk', 'ulys'))
- grad_upproj: float32 [768, 3072], P(('blk', 'ulys'))
- grad_upbias: float32 [3072], P(('blk', 'ulys'))
- grad_downproj: float32 [3072, 768], P(('blk', 'ulys'))
- grad_downbias: float32 [768], P(('blk', 'ulys'))
- prenorm_gain_gradient: float32 [768], P(('blk', 'ulys'))
- prenorm_shift_gradient: float32 [768], P(('blk', 'ulys'))
- grad_mlpgain: float32 [768], P(('blk', 'ulys'))
- grad_mlpshift: float32 [768], P(('blk', 'ulys'))
Inputs may be any that keep to these rules, and one draw needn't show every extreme that they name: `segment_ids`: segment ids never fall along a sequence; a document holds at most 384 tokens, and some document of each sequence holds exactly that many.
All inputs are finite; a program needn't handle non-finite values. No bound on the sum of `key_valid` on one device may be relied on, other than what follows from the above.
Results may differ from a plain program's by a relative error of at most 0.0003.
Values sent between devices are 32-bit elements; how exact they have to be, the bound alone decides.
No kernel may reach another device: no remote copies, remote signals or barrier semaphores. Data moves between devices by JAX's collectives and lax.ppermute only.
A program may use at most 192 MiB of HBM per device.

v0:
```python
import math
import jax
import jax.numpy as jnp
from jax import lax
from jax.sharding import PartitionSpec as P

HEAD_DIM = 64
HIGH = lax.Precision.HIGHEST
floor_score = -1e30


def layer_normalize(values, gain, shift):
    average = jnp.mean(values, axis=-1, keepdims=True)
    centred = values - average
    variance = jnp.mean(centred * centred, axis=-1, keepdims=True)
    return centred * lax.rsqrt(variance + 1e-05) * gain + shift


def gelu_tanh(values):
    return (
        0.5
        * values
        * (1.0 + jnp.tanh(0.7978845608028654 * (values + 0.044715 * values * values * values)))
    )


def matmul(left, right):
    return jnp.dot(left, right, precision=HIGH)


def matmul_left_t(left, right):
    return lax.dot_general(left, right, (((0,), (0,)), ((), ())), precision=HIGH)


def matmul_right_t(left, right):
    return lax.dot_general(left, right, (((1,), (1,)), ((), ())), precision=HIGH)


def local(
    hidden,
    time_embed,
    segment_ids,
    key_valid,
    out_grad,
    w_query,
    b_query,
    w_key,
    w_value,
    b_value,
    w_out,
    b_out,
    w_up,
    b_up,
    w_down,
    b_down,
    pre_gain,
    pre_shift,
    mlp_gain,
    mlp_shift,
):
    (
        full_query,
        full_qbias,
        full_key,
        full_value,
        full_vbias,
        full_out,
        full_obias,
        full_up,
        full_upbias,
        full_down,
        full_downbias,
        complete_prenorm_gain,
        complete_prenorm_shift,
        full_mlpgain,
        full_mlpshift,
    ) = (
        lax.all_gather(w_query, ("blk", "ulys"), axis=0, tiled=True),
        lax.all_gather(b_query, ("blk", "ulys"), axis=0, tiled=True),
        lax.all_gather(w_key, ("blk", "ulys"), axis=0, tiled=True),
        lax.all_gather(w_value, ("blk", "ulys"), axis=0, tiled=True),
        lax.all_gather(b_value, ("blk", "ulys"), axis=0, tiled=True),
        lax.all_gather(w_out, ("blk", "ulys"), axis=0, tiled=True),
        lax.all_gather(b_out, ("blk", "ulys"), axis=0, tiled=True),
        lax.all_gather(w_up, ("blk", "ulys"), axis=0, tiled=True),
        lax.all_gather(b_up, ("blk", "ulys"), axis=0, tiled=True),
        lax.all_gather(w_down, ("blk", "ulys"), axis=0, tiled=True),
        lax.all_gather(b_down, ("blk", "ulys"), axis=0, tiled=True),
        lax.all_gather(pre_gain, ("blk", "ulys"), axis=0, tiled=True),
        lax.all_gather(pre_shift, ("blk", "ulys"), axis=0, tiled=True),
        lax.all_gather(mlp_gain, ("blk", "ulys"), axis=0, tiled=True),
        lax.all_gather(mlp_shift, ("blk", "ulys"), axis=0, tiled=True),
    )
    residual_input = hidden + time_embed
    normalized_rows, prenorm_backward = jax.vjp(
        layer_normalize, residual_input, complete_prenorm_gain, complete_prenorm_shift
    )
    query = matmul(normalized_rows, full_query) + full_qbias
    keys = matmul(normalized_rows, full_key)
    values = matmul(normalized_rows, full_value) + full_vbias
    query_heads, key_heads, value_heads = (
        lax.all_to_all(query, "ulys", split_axis=1, concat_axis=0, tiled=True),
        lax.all_to_all(keys, "ulys", split_axis=1, concat_axis=0, tiled=True),
        lax.all_to_all(values, "ulys", split_axis=1, concat_axis=0, tiled=True),
    )
    group = query_heads.shape[0]
    width = query_heads.shape[1]
    heads_here = width // HEAD_DIM
    blk_count = lax.axis_size("blk")
    blk_here = lax.axis_index("blk")
    length = group * blk_count
    scale = HEAD_DIM ** (-0.5)
    segments_here = segment_ids[0]
    query_codes = segments_here.astype(jnp.float32)
    key_codes = jnp.where(key_valid[0] == 1, segments_here, -1).astype(jnp.float32)
    query_rows = blk_here * group + jnp.arange(group, dtype=jnp.int32)
    query_split = query_heads.reshape(group, heads_here, HEAD_DIM)
    key_value = jnp.concatenate([key_heads, value_heads], axis=1)

    def block_scores(kv_block, code_block, key_rows):
        key_split = kv_block[:, :width].reshape(-1, heads_here, HEAD_DIM)
        value_split = kv_block[:, width:].reshape(-1, heads_here, HEAD_DIM)
        scores = jnp.einsum("qhd,khd->hqk", query_split, key_split, precision=HIGH) * scale
        allowed = (query_codes[:, None] == code_block[None, :]) | (
            query_rows[:, None] == key_rows[None, :]
        )
        return (scores, allowed[None], key_split, value_split)

    def over_blocks(state, piece, update):
        kv_piece, code_piece = piece
        rows = kv_piece.shape[0]
        size = math.gcd(rows, group)
        count = rows // size
        kv_blocks = kv_piece.reshape(count, size, kv_piece.shape[1])
        code_blocks = code_piece.reshape(count, size)
        offsets = jnp.arange(count, dtype=jnp.int32) * size

        def visit(carried, item):
            kv_block, code_block, offset = item
            key_rows = offset + jnp.arange(size, dtype=jnp.int32)
            carried = update(carried, kv_block, code_block, key_rows)
            return (carried, None)

        state, unused = lax.scan(visit, state, (kv_blocks, code_blocks, offsets))
        return state

    def forward_update(state, kv_block, code_block, key_rows):
        running_max, total, accum = state
        scores, allowed, key_split, value_split = block_scores(kv_block, code_block, key_rows)
        masked = jnp.where(allowed, scores, floor_score)
        new_max = jnp.maximum(running_max, jnp.max(masked, axis=2))
        weights = jnp.where(allowed, jnp.exp(masked - new_max[:, :, None]), 0.0)
        factor = jnp.exp(running_max - new_max)
        total = total * factor + jnp.sum(weights, axis=2)
        weighted = jnp.einsum("hqk,khd->qhd", weights, value_split, precision=HIGH)
        accum = accum.reshape(group, heads_here, HEAD_DIM) * factor.T[:, :, None] + weighted
        return (new_max, total, accum.reshape(group, width))

    start_state = (
        jnp.full((heads_here, group), floor_score, jnp.float32),
        jnp.zeros((heads_here, group), jnp.float32),
        jnp.zeros((group, width), jnp.float32),
    )
    running_max, total, accum = over_blocks(
        start_state,
        (
            lax.all_gather(key_value, "blk", axis=0, tiled=True),
            lax.all_gather(key_codes, "blk", axis=0, tiled=True),
        ),
        forward_update,
    )
    normalizer = running_max + jnp.log(total)
    attended_heads = (accum.reshape(group, heads_here, HEAD_DIM) / total.T[:, :, None]).reshape(
        group, width
    )
    attended = lax.all_to_all(attended_heads, "ulys", split_axis=0, concat_axis=1, tiled=True)
    middle = residual_input + matmul(attended, full_out) + full_obias
    mlp_in, mlp_back = jax.vjp(layer_normalize, middle, full_mlpgain, full_mlpshift)
    pre_act = matmul(mlp_in, full_up) + full_upbias
    activated, gelu_back = jax.vjp(gelu_tanh, pre_act)
    output = middle + matmul(activated, full_down) + full_downbias
    back_query, back_key, back_value, back_out, back_up, back_down = (
        lax.all_gather(w_query, ("blk", "ulys"), axis=0, tiled=True),
        lax.all_gather(w_key, ("blk", "ulys"), axis=0, tiled=True),
        lax.all_gather(w_value, ("blk", "ulys"), axis=0, tiled=True),
        lax.all_gather(w_out, ("blk", "ulys"), axis=0, tiled=True),
        lax.all_gather(w_up, ("blk", "ulys"), axis=0, tiled=True),
        lax.all_gather(w_down, ("blk", "ulys"), axis=0, tiled=True),
    )
    grad_downbias = jnp.sum(out_grad, axis=0)
    grad_downproj = matmul_left_t(activated, out_grad)
    act_grad = matmul_right_t(out_grad, back_down)
    (pre_grad,) = gelu_back(act_grad)
    grad_upproj = matmul_left_t(mlp_in, pre_grad)
    grad_upbias = jnp.sum(pre_grad, axis=0)
    mlp_in_grad = matmul_right_t(pre_grad, back_up)
    middle_part, grad_mlpgain, grad_mlpshift = mlp_back(mlp_in_grad)
    middle_grad = out_grad + middle_part
    grad_outproj = matmul_left_t(attended, middle_grad)
    grad_obias = jnp.sum(middle_grad, axis=0)
    attended_grad = matmul_right_t(middle_grad, back_out)
    grad_heads = lax.all_to_all(attended_grad, "ulys", split_axis=1, concat_axis=0, tiled=True)
    grad_split = grad_heads.reshape(group, heads_here, HEAD_DIM)
    row_dots = jnp.sum(grad_split * attended_heads.reshape(group, heads_here, HEAD_DIM), axis=2).T

    def backward_from(first_row):

        def backward_update(state, kv_block, code_block, key_rows):
            query_grad, pair_grads = state
            scores, allowed, key_split, value_split = block_scores(kv_block, code_block, key_rows)
            weights = jnp.exp(jnp.where(allowed, scores - normalizer[:, :, None], floor_score))
            values_grad = jnp.einsum("hqk,qhd->khd", weights, grad_split, precision=HIGH)
            weights_grad = jnp.einsum("qhd,khd->hqk", grad_split, value_split, precision=HIGH)
            score_grad = weights * (weights_grad - row_dots[:, :, None]) * scale
            query_grad = query_grad + jnp.einsum(
                "hqk,khd->qhd", score_grad, key_split, precision=HIGH
            ).reshape(group, width)
            keys_grad = jnp.einsum("hqk,qhd->khd", score_grad, query_split, precision=HIGH)
            size = key_rows.shape[0]
            block_grad = jnp.concatenate(
                [keys_grad.reshape(size, width), values_grad.reshape(size, width)], axis=1
            )
            place = key_rows[0] - first_row
            current = lax.dynamic_slice_in_dim(pair_grads, place, size, 0)
            pair_grads = lax.dynamic_update_slice_in_dim(pair_grads, current + block_grad, place, 0)
            return (query_grad, pair_grads)

        return backward_update

    back_state = (
        jnp.zeros((group, width), jnp.float32),
        jnp.zeros((length, 2 * width), jnp.float32),
    )
    query_grad, pair_grads = over_blocks(
        back_state,
        (
            lax.all_gather(key_value, "blk", axis=0, tiled=True),
            lax.all_gather(key_codes, "blk", axis=0, tiled=True),
        ),
        backward_from(0),
    )
    local_pairs = lax.psum_scatter(pair_grads, "blk", scatter_dimension=0, tiled=True)
    token_query_grad, token_keys_grad, token_values_grad = (
        lax.all_to_all(query_grad, "ulys", split_axis=0, concat_axis=1, tiled=True),
        lax.all_to_all(local_pairs[:, :width], "ulys", split_axis=0, concat_axis=1, tiled=True),
        lax.all_to_all(local_pairs[:, width:], "ulys", split_axis=0, concat_axis=1, tiled=True),
    )
    grad_query = matmul_left_t(normalized_rows, token_query_grad)
    grad_qbias = jnp.sum(token_query_grad, axis=0)
    grad_key = matmul_left_t(normalized_rows, token_keys_grad)
    grad_value = matmul_left_t(normalized_rows, token_values_grad)
    grad_vbias = jnp.sum(token_values_grad, axis=0)
    normalized_gradient = (
        matmul_right_t(token_query_grad, back_query)
        + matmul_right_t(token_keys_grad, back_key)
        + matmul_right_t(token_values_grad, back_value)
    )
    residual_slice, prenorm_gain_gradient, prenorm_shift_gradient = prenorm_backward(
        normalized_gradient
    )
    hidden_grad = middle_grad + residual_slice
    shard_sums = (
        lax.psum_scatter(grad_query, ("blk", "ulys"), scatter_dimension=0, tiled=True),
        lax.psum_scatter(grad_qbias, ("blk", "ulys"), scatter_dimension=0, tiled=True),
        lax.psum_scatter(grad_key, ("blk", "ulys"), scatter_dimension=0, tiled=True),
        lax.psum_scatter(grad_value, ("blk", "ulys"), scatter_dimension=0, tiled=True),
        lax.psum_scatter(grad_vbias, ("blk", "ulys"), scatter_dimension=0, tiled=True),
        lax.psum_scatter(grad_outproj, ("blk", "ulys"), scatter_dimension=0, tiled=True),
        lax.psum_scatter(grad_obias, ("blk", "ulys"), scatter_dimension=0, tiled=True),
        lax.psum_scatter(grad_upproj, ("blk", "ulys"), scatter_dimension=0, tiled=True),
        lax.psum_scatter(grad_upbias, ("blk", "ulys"), scatter_dimension=0, tiled=True),
        lax.psum_scatter(grad_downproj, ("blk", "ulys"), scatter_dimension=0, tiled=True),
        lax.psum_scatter(grad_downbias, ("blk", "ulys"), scatter_dimension=0, tiled=True),
        lax.psum_scatter(prenorm_gain_gradient, ("blk", "ulys"), scatter_dimension=0, tiled=True),
        lax.psum_scatter(prenorm_shift_gradient, ("blk", "ulys"), scatter_dimension=0, tiled=True),
        lax.psum_scatter(grad_mlpgain, ("blk", "ulys"), scatter_dimension=0, tiled=True),
        lax.psum_scatter(grad_mlpshift, ("blk", "ulys"), scatter_dimension=0, tiled=True),
    )
    totals = lax.psum(
        (
            shard_sums[0],
            shard_sums[1],
            shard_sums[2],
            shard_sums[3],
            shard_sums[4],
            shard_sums[5],
            shard_sums[6],
            shard_sums[7],
            shard_sums[8],
            shard_sums[9],
            shard_sums[10],
            shard_sums[11],
            shard_sums[12],
            shard_sums[13],
            shard_sums[14],
        ),
        "dp",
    )
    return (output, hidden_grad) + tuple(totals)


def solution(mesh):
    placed = (
        P(("dp", "blk", "ulys"), None),
        P("dp", None),
        P("dp", "blk"),
        P("dp", "blk"),
        P(("dp", "blk", "ulys"), None),
        P(("blk", "ulys"), None),
        P(("blk", "ulys")),
        P(("blk", "ulys"), None),
        P(("blk", "ulys"), None),
        P(("blk", "ulys")),
        P(("blk", "ulys"), None),
        P(("blk", "ulys")),
        P(("blk", "ulys"), None),
        P(("blk", "ulys")),
        P(("blk", "ulys"), None),
        P(("blk", "ulys")),
        P(("blk", "ulys")),
        P(("blk", "ulys")),
        P(("blk", "ulys")),
        P(("blk", "ulys")),
    )
    return jax.shard_map(
        local,
        mesh=mesh,
        in_specs=placed,
        out_specs=(
            P(("dp", "blk", "ulys"), None),
            P(("dp", "blk", "ulys"), None),
            P(("blk", "ulys"), None),
            P(("blk", "ulys")),
            P(("blk", "ulys"), None),
            P(("blk", "ulys"), None),
            P(("blk", "ulys")),
            P(("blk", "ulys"), None),
            P(("blk", "ulys")),
            P(("blk", "ulys"), None),
            P(("blk", "ulys")),
            P(("blk", "ulys"), None),
            P(("blk", "ulys")),
            P(("blk", "ulys")),
            P(("blk", "ulys")),
            P(("blk", "ulys")),
            P(("blk", "ulys")),
        ),
        check_vma=False,
    )
```

profile of v0, /device:TPU:0, one launch (start us, length us, event | category | flops | bytes accessed | tf_op | source)
XLA Modules:
  0.0 1022.3 jit_solution(7947573977653093022)
XLA Ops:
  18.0 26.4 %all-reduce.18 = (f32[768]{0:T(1024)S(1)}, f32[768]{0:T(1024)S(1)}, f32[768]{0:T(1024)S(1)}, f32[768]{0:T(1024)}, f32[768]{0:T(1024)}, /*index=5*/f32[768]{0:T(1024)}, f32[768]{0:T(1024)}) all-reduce(f32[768]{0:T(1024)S(1)} %dynamic-update-slice.2, ...), channel_id=1, replica_groups=mesh['dp'=4,'blk'=2,'ulys'=4] {'blk','ulys'}, use_global_device_ids=true, to_apply=%add.2 | all-reduce | flops 5376 | bytes 43008
  55.1 19.6 %all-gather.10.cloned.1.call-done = f32[768,768]{1,0:T(8,128)} async-done(((f32[96,768]{1,0:T(8,128)}), f32[768,768]{1,0:T(8,128)}) %all-gather.10.cloned.1.call-update) | async-done | bytes 2359312 | tf_op jit(solution)/shard_map/all_gather | solution.py:80
  85.7 12.1 %all-to-all-done = f32[192,4,192]{0,2,1:T(8,128)S(1)} async-done(((f32[192,4,192]{0,2,1:T(8,128)}), f32[192,4,192]{0,2,1:T(8,128)S(1)}, u32[]{:S(2)}, u32[]{:S(2)}) %all-to-all-start) | async-done | bytes 589856 | tf_op jit(solution)/shard_map/all_to_all | solution.py:103
  129.3 16.9 %all-gather.14.cloned.1.call-done = f32[1536,384]{0,1:T(8,128)} async-done(((f32[768,384]{0,1:T(8,128)}), f32[1536,384]{0,1:T(8,128)}) %all-gather.14.cloned.1.call-update) | async-done | bytes 2359312 | tf_op jit(solution)/shard_map/all_gather | solution.py:167
  150.3 49.9 %while.28 = (s32[]{:T(128)}, f32[3,768]{1,0:T(4,128)S(1)}, f32[3,768]{1,0:T(4,128)}, f32[768,192]{0,1:T(8,128)S(1)}, f32[768]{0:T(1024)}, /*index=5*/f32[2,768]{...) while((s32[]{:T(128)}, f32[3,768]{1,0:T(4,128)S(1)}, ...), condition=%wide.region_5.6_spmd.clone, body=%wide.region_2.5_spmd.clone.sunk | while | flops 2741222400 | bytes 31506652 | solution.py:144
  205.9 22.6 %all-gather.1 = f32[8,1,384]{2,1,0:T(1,128)} all-gather(f32[1,1,384]{2,1,0:T(1,128)S(1)} %reshape.337), channel_id=1, replica_groups=mesh['dp'=4,'blk'=2,'ulys'=4] {'blk','ulys'}, dimensions={0}, use_global_device_ids=true | all-gather | bytes 13824 | tf_op jit(solution)/shard_map/all_gather | solution.py:86
  234.9 10.0 all-gather.20.cloned.1.call-done
  244.9 9.0 convolution_add_fusion
  254.0 50.8 %all-gather.22.cloned.1.call-done = f32[3072,768]{1,0:T(8,128)} async-done(((f32[384,768]{1,0:T(8,128)}), f32[3072,768]{1,0:T(8,128)}) %all-gather.22.cloned.1.call-update) | async-done | bytes 9437200 | tf_op jit(solution)/shard_map/all_gather | solution.py:87
  304.7 14.4 %fusion.64 = (f32[3072]{0:T(1024)}, f32[192,3072]{1,0:T(8,128)S(1)}) fusion(f32[192,3072]{1,0:T(8,128)S(1)} %convolution_add_fusion, f32[192,768]{1,0:T(8,128)} %param.28, f32[3072,768]{1,0:T(8,128)} %all-gather.22.cloned.1.call-done), kind=kOutput, calls=%fused_computation.123 | convolution fusion | flops 5449970688 | bytes 14757888 | tf_op jit(solution)/shard_map/dot_general | solution.py:36
  319.2 10.1 multiply_reduce_fusion
  340.4 11.0 %all-to-all-done.4 = f32[192,4,192]{2,0,1:T(8,128)} async-done(((f32[192,4,192]{2,0,1:T(8,128)}), f32[192,4,192]{2,0,1:T(8,128)}, u32[]{:S(2)}, u32[]{:S(2)}) %all-to-all-start.4) | async-done | bytes 589856 | tf_op jit(solution)/shard_map/all_to_all | solution.py:202
  357.8 123.8 %while.29 = (s32[]{:T(128)}, f32[768,192]{0,1:T(8,128)S(1)}, f32[1536,384]{0,1:T(8,128)}, f32[2,768,384]{1,2,0:T(8,128)}, f32[768]{0:T(1024)S(1)}, /*index=5*/f3...) while((s32[]{:T(128)}, f32[768,192]{0,1:T(8,128)S(1)}, ...), condition=%wide.region_12.13_spmd.clone, body=%wide.region_11.12_spmd.clone.sunk | while | flops 6813353472 | bytes 72011080 | solution.py:144
  390.5 8.8 fusion.165
  399.4 8.7 fusion.163
  439.0 8.8 fusion.165
  447.8 8.7 fusion.163
  486.8 14.1 %all_to_all.146 = f32[4,192,192]{2,1,0:T(8,128)S(1)} all-to-all(f32[4,192,192]{2,1,0:T(8,128)S(1)} %bitcast.210), channel_id=1, replica_groups=mesh['dp'=4,'blk'=2,'ulys'=4] {'ulys'}, dimensions={0} | all-to-all | bytes 1179648 | tf_op jit(solution)/shard_map/all_to_all | solution.py:244
  506.5 10.0 reduce-scatter.8.cloned.1.call-done
  518.1 14.2 %all_to_all.147 = f32[4,192,192]{2,1,0:T(8,128)S(1)} all-to-all(f32[4,192,192]{2,1,0:T(8,128)S(1)} %bitcast.211), channel_id=1, replica_groups=mesh['dp'=4,'blk'=2,'ulys'=4] {'ulys'}, dimensions={0} | all-to-all | bytes 1179648 | tf_op jit(solution)/shard_map/all_to_all | solution.py:246
  538.2 20.1 %all_to_all.148 = f32[4,192,192]{2,1,0:T(8,128)S(1)} all-to-all(f32[4,192,192]{2,1,0:T(8,128)S(1)} %bitcast.212), channel_id=1, replica_groups=mesh['dp'=4,'blk'=2,'ulys'=4] {'ulys'}, dimensions={0} | all-to-all | bytes 1179648 | tf_op jit(solution)/shard_map/all_to_all | solution.py:245
  565.1 10.9 %fusion.37 = f32[768,3072]{1,0:T(8,128)} fusion(f32[192,3072]{1,0:T(8,128)S(1)} %copy-done.13, f32[192,768]{1,0:T(8,128)S(1)} %copy-done.6, f32[768]{0:T(1024)S(1)} %copy-done.36, f32[768]{0:T(1024)S(1)} %copy-done.35, f32[192]{0:T(256)} %fusion.50, f32[192]{0:T(256)} %copy-done.40), kind=kOutput, calls=%fused_computation.82 | convolution fusion | flops 5436407808 | bytes 12393984 | tf_op jit(solution)/shard_map/dot_general | solution.py:32
  577.7 11.7 %fusion.36 = f32[3072,768]{1,0:T(8,128)} fusion(f32[192,768]{1,0:T(8,128)} %param.28, f32[192,3072]{1,0:T(8,128)S(1)} %copy-done.3), kind=kOutput, calls=%fused_computation.65 | convolution fusion | flops 5440536576 | bytes 12386304 | tf_op jit(solution)/shard_map/dot_general | solution.py:32
  589.5 25.1 %reduce-scatter.10.cloned.1.call-done = f32[96,768]{1,0:T(8,128)} async-done(((f32[768,768]{1,0:T(8,128)}), f32[96,768]{1,0:T(8,128)}) %reduce-scatter.10.cloned.1.call-update) | async-done | bytes 294928 | tf_op jit(solution)/shard_map/reduce_scatter | solution.py:263
  614.6 46.2 %reduce-scatter.14.cloned.1.call-done = f32[96,768]{1,0:T(8,128)} async-done(((f32[768,768]{1,0:T(8,128)}), f32[96,768]{1,0:T(8,128)}) %reduce-scatter.14.cloned.1.call-update) | async-done | bytes 294928 | tf_op jit(solution)/shard_map/reduce_scatter | solution.py:266
  660.8 45.7 %reduce-scatter.12.cloned.1.call-done = f32[96,768]{1,0:T(8,128)} async-done(((f32[768,768]{1,0:T(8,128)}), f32[96,768]{1,0:T(8,128)}) %reduce-scatter.12.cloned.1.call-update) | async-done | bytes 294928 | tf_op jit(solution)/shard_map/reduce_scatter | solution.py:265
  706.5 80.4 %reduce-scatter.18.cloned.1.call-done = f32[96,3072]{1,0:T(8,128)} async-done(((f32[768,3072]{1,0:T(8,128)}), f32[96,3072]{1,0:T(8,128)}) %reduce-scatter.18.cloned.1.call-update) | async-done | bytes 1179664 | tf_op jit(solution)/shard_map/reduce_scatter | solution.py:270
  787.0 80.3 %reduce-scatter.20.cloned.1.call-done = f32[384,768]{1,0:T(8,128)} async-done(((f32[3072,768]{1,0:T(8,128)}), f32[384,768]{1,0:T(8,128)}) %reduce-scatter.20.cloned.1.call-update) | async-done | bytes 1179664 | tf_op jit(solution)/shard_map/reduce_scatter | solution.py:272
  888.4 26.3 %all-reduce.17 = (f32[768]{0:T(1024)}, f32[768]{0:T(1024)}, f32[768]{0:T(1024)}, f32[768]{0:T(1024)}, f32[3072]{0:T(1024)}, /*index=5*/f32[768]{0:T(1024)}, f32[...) all-reduce(f32[768]{0:T(1024)} %dynamic-update-slice.7, ...), channel_id=1, replica_groups=mesh['dp'=4,'blk'=2,'ulys'=4] {'blk','ulys'}, use_global_device_ids=true, to_apply=%add.7 | all-reduce | flops 9984 | bytes 79872
  926.1 13.0 %all-reduce.19 = (f32[96]{0:T(128)}, f32[96]{0:T(128)}, f32[96]{0:T(128)}, f32[384]{0:T(512)}, f32[96]{0:T(128)}, /*index=5*/f32[96]{0:T(128)}, f32[96]{0:T(128)}, f32[96]{0:T(128)}, f32[96]{0:T(128)}) all-reduce(f32[96]{0:T(128)} %dynamic-slice.9, f32[96]{0:T(128)} %dynamic-slice.11, ...), channel_id=1, replica_groups=mesh['dp'=4,'blk'=2,'ulys'=4] {'dp'}, use_global_device_ids=true, to_apply=%region_20.21 | all-reduce | flops 1152 | bytes 9216 | tf_op jit(solution)/shard_map/psum | solution.py:279
  943.3 10.4 %fusion.35 = f32[192,768]{1,0:T(8,128)} fusion(f32[192,768]{1,0:T(8,128)S(1)} %copy-done.6, f32[3072,768]{1,0:T(8,128)} %all-gather.22.cloned.1.call-done, f32[192,3072]{1,0:T(8,128)S(1)} %copy-done.3, f32[768]{0:T(1024)S(1)} %copy-done.51), kind=kOutput, calls=%fused_computation.63 | convolution fusion | flops 5440831488 | bytes 12979200 | tf_op jit(solution)/shard_map/dot_general | solution.py:28
  953.6 52.7 %all-reduce.23.cloned.1.call-done = (f32[96,768]{1,0:T(8,128)}, f32[96,768]{1,0:T(8,128)}, f32[96,768]{1,0:T(8,128)}, f32[96,768]{1,0:T(8,128)}, f32[96,3072]{1,0:T(8,128)}, /*index=5*/f32[384,768]{1,0:T(8,128)}) async-done(((f32[96,768]{1,0:T(8,128)}, f32[96,768]{1,0:T(8,128)}, f32[96,768]{1,0:T(8,128)}, f32[96,768]{1,0:T(8,128)}, f32[96,3072]{1,0:T(8,128)}, /*index=5*/f32[384,768]{1,0:T(8,128)}), ...) | async-done | bytes 3538960 | tf_op jit(solution)/shard_map/psum | solution.py:279
  (334 shorter events, 265.8 us)
Async XLA Ops:
  7.2 39.7 %copy-start = (f32[192,768]{1,0:T(8,128)S(1)}, f32[192,768]{1,0:T(8,128)}, u32[]{:S(2)}) copy-start(f32[192,768]{1,0:T(8,128)} %param.24) | copy-start | bytes 1769476
  7.2 39.7 %all-gather.12.cloned.1.call-start = ((), (), s32[]{:S(2)}) async-start(), calls=%async_computation.16 | async-start | bytes 2654208 | tf_op jit(solution)/shard_map/all_gather | solution.py:81
  7.9 66.7 %all-gather.10.cloned.1.call-start = ((), (), s32[]{:S(2)}) async-start(), calls=%async_computation.15 | async-start | bytes 2654208 | tf_op jit(solution)/shard_map/all_gather | solution.py:80
  8.7 99.4 %all-gather.16.cloned.1.call-start = ((), (), s32[]{:S(2)}) async-start(), calls=%async_computation.18 | async-start | bytes 2654208 | tf_op jit(solution)/shard_map/all_gather | solution.py:78
  44.4 30.3 %copy-start.31 = (f32[768]{0:T(1024)}, f32[768]{0:T(1024)S(1)}, u32[]{:S(2)}) copy-start(f32[768]{0:T(1024)S(1)} %get-tuple-element.345) | copy-start | bytes 9220
  44.4 30.3 %copy-start.37 = (f32[768]{0:T(1024)}, f32[768]{0:T(1024)S(1)}, u32[]{:S(2)}) copy-start(f32[768]{0:T(1024)S(1)} %get-tuple-element.344) | copy-start | bytes 9220
  45.6 29.1 %copy-start.42 = (f32[192]{0:T(256)}, f32[192]{0:T(256)S(1)}, u32[]{:S(2)}) copy-start(f32[192]{0:T(256)S(1)} %broadcast_multiply_fusion.1) | copy-start | bytes 2308
  46.9 27.8 %copy-start.47 = (f32[192]{0:T(256)}, f32[192]{0:T(256)S(1)}, u32[]{:S(2)}) copy-start(f32[192]{0:T(256)S(1)} %fusion.49) | copy-start | bytes 2308
  51.6 29.5 %all-to-all-start.1 = ((f32[192,4,192]{0,2,1:T(8,128)}), f32[192,4,192]{0,2,1:T(8,128)S(1)}, u32[]{:S(2)}, u32[]{:S(2)}) async-start(f32[192,4,192]{0,2,1:T(8,128)} %bitcast.3), calls=%async_computation.1 | async-start | bytes 1572864 | tf_op jit(solution)/shard_map/all_to_all | solution.py:104
  81.1 16.7 %all-to-all-start = ((f32[192,4,192]{0,2,1:T(8,128)}), f32[192,4,192]{0,2,1:T(8,128)S(1)}, u32[]{:S(2)}, u32[]{:S(2)}) async-start(f32[192,4,192]{0,2,1:T(8,128)} %bitcast.1), calls=%async_computation | async-start | bytes 1572864 | tf_op jit(solution)/shard_map/all_to_all | solution.py:103
  84.6 61.6 %all-gather.14.cloned.1.call-start = ((), (), s32[]{:S(2)}) async-start(), calls=%async_computation.17 | async-start | bytes 3538944 | tf_op jit(solution)/shard_map/all_gather | solution.py:167
  99.9 129.6 %all-gather.18.cloned.1.call-start = ((), (), s32[]{:S(2)}) async-start(), calls=%async_computation.19 | async-start | bytes 2654208 | tf_op jit(solution)/shard_map/all_gather | solution.py:83
  100.5 144.4 %all-gather.20.cloned.1.call-start = ((), (), s32[]{:S(2)}) async-start(), calls=%async_computation.20 | async-start | bytes 10616832 | tf_op jit(solution)/shard_map/all_gather | solution.py:85
  101.1 203.6 %all-gather.22.cloned.1.call-start = ((), (), s32[]{:S(2)}) async-start(), calls=%async_computation.21 | async-start | bytes 10616832 | tf_op jit(solution)/shard_map/all_gather | solution.py:87
  113.2 15.2 %all-to-all-start.2 = ((f32[192,4,192]{2,0,1:T(8,128)}), f32[192,4,192]{2,0,1:T(8,128)S(1)}, u32[]{:S(2)}, u32[]{:S(2)}) async-start(f32[192,4,192]{2,0,1:T(8,128)} %copy.98), calls=%async_computation.2 | async-start | bytes 1572864 | tf_op jit(solution)/shard_map/all_to_all | solution.py:102
  200.2 28.3 %copy-start.19 = (f32[768,192]{0,1:T(8,128)}, f32[768,192]{0,1:T(8,128)S(1)}, u32[]{:S(2)}) copy-start(f32[768,192]{0,1:T(8,128)S(1)} %get-tuple-element.134) | copy-start | bytes 1769476
  202.2 27.3 %copy-start.56 = (f32[768]{0:T(1024)S(1)}, f32[768]{0:T(1024)}, u32[]{:S(2)}) copy-start(f32[768]{0:T(1024)} %get-tuple-element.347) | copy-start | bytes 9220
  202.2 26.3 %all-to-all-start.3 = ((f32[4,192,192]{2,1,0:T(8,128)}), f32[4,192,192]{2,1,0:T(8,128)S(1)}, u32[]{:S(2)}, u32[]{:S(2)}) async-start(f32[4,192,192]{2,1,0:T(8,128)} %bitcast.9), calls=%async_computation.3 | async-start | bytes 1572864 | tf_op jit(solution)/shard_map/all_to_all | solution.py:176
  253.9 65.2 %copy-start.2 = (f32[192,3072]{1,0:T(8,128)}, f32[192,3072]{1,0:T(8,128)S(1)}, u32[]{:S(2)}) copy-start(f32[192,3072]{1,0:T(8,128)S(1)} %convolution_add_fusion) | copy-start | bytes 7077892
  335.4 20.0 %copy-start.20 = (f32[768,192]{0,1:T(8,128)S(1)}, f32[768,192]{0,1:T(8,128)}, u32[]{:S(2)}) copy-start(f32[768,192]{0,1:T(8,128)} %copy-done.19) | copy-start | bytes 1769476
  335.4 16.1 %all-to-all-start.4 = ((f32[192,4,192]{2,0,1:T(8,128)}), f32[192,4,192]{2,0,1:T(8,128)}, u32[]{:S(2)}, u32[]{:S(2)}) async-start(f32[192,4,192]{2,0,1:T(8,128)} %copy.103), calls=%async_computation.4 | async-start | bytes 1572864 | tf_op jit(solution)/shard_map/all_to_all | solution.py:202
  339.7 176.8 %reduce-scatter.8.cloned.1.call-start = ((), (), s32[]{:S(2)}) async-start(), calls=%async_computation.22 | async-start | bytes 3538944 | tf_op jit(solution)/shard_map/reduce_scatter | solution.py:242
  481.6 107.9 %reduce-scatter.16.cloned.1.call-start = ((), (), s32[]{:S(2)}) async-start(), calls=%async_computation.26 | async-start | bytes 2654208 | tf_op jit(solution)/shard_map/reduce_scatter | solution.py:268
  486.4 128.2 %reduce-scatter.10.cloned.1.call-start = ((), (), s32[]{:S(2)}) async-start(), calls=%async_computation.23 | async-start | bytes 2654208 | tf_op jit(solution)/shard_map/reduce_scatter | solution.py:263
  486.7 16.0 %copy-start.33 = (f32[768]{0:T(1024)S(1)}, f32[768]{0:T(1024)}, u32[]{:S(2)}) copy-start(f32[768]{0:T(1024)} %copy-done.31) | copy-start | bytes 9220
  486.7 16.0 %copy-start.39 = (f32[768]{0:T(1024)S(1)}, f32[768]{0:T(1024)}, u32[]{:S(2)}) copy-start(f32[768]{0:T(1024)} %copy-done.37) | copy-start | bytes 9220
  506.4 154.4 %reduce-scatter.14.cloned.1.call-start = ((), (), s32[]{:S(2)}) async-start(), calls=%async_computation.25 | async-start | bytes 2654208 | tf_op jit(solution)/shard_map/reduce_scatter | solution.py:266
  537.8 168.7 %reduce-scatter.12.cloned.1.call-start = ((), (), s32[]{:S(2)}) async-start(), calls=%async_computation.24 | async-start | bytes 2654208 | tf_op jit(solution)/shard_map/reduce_scatter | solution.py:265
  565.0 222.0 %reduce-scatter.18.cloned.1.call-start = ((), (), s32[]{:S(2)}) async-start(), calls=%async_computation.27 | async-start | bytes 10616832 | tf_op jit(solution)/shard_map/reduce_scatter | solution.py:270
  576.0 291.3 %reduce-scatter.20.cloned.1.call-start = ((), (), s32[]{:S(2)}) async-start(), calls=%async_computation.28 | async-start | bytes 10616832 | tf_op jit(solution)/shard_map/reduce_scatter | solution.py:272
  589.4 279.8 %copy-start.60 = (f32[96]{0:T(128)S(1)}, f32[96]{0:T(128)}, u32[]{:S(2)}) copy-start(f32[96]{0:T(128)} %param.39) | copy-start | bytes 1156
  589.4 416.9 %all-reduce.23.cloned.1.call-start = ((), (), s32[]{:S(2)}) async-start(), calls=%async_computation.29 | async-start | bytes 7077888 | tf_op jit(solution)/shard_map/psum | solution.py:279
  (55 other events, 353.4 us)
Sparse Core Ops, SparseCore 0:
  9.9 32.0 all-gather.11
  43.9 30.6 all-gather.9
  76.5 31.5 all-gather.15
  110.1 36.0 all-gather.13
  147.9 29.0 all-gather.17
  178.8 66.0 all-gather.19
  246.8 57.9 all-gather.21
  481.7 34.7 reduce-scatter.7
  520.2 48.6 reduce-scatter.15
  572.1 42.4 reduce-scatter.9
  618.3 42.4 reduce-scatter.13
  664.0 42.4 reduce-scatter.11
  710.4 76.4 reduce-scatter.17
  790.7 76.4 reduce-scatter.19
  870.2 136.1 all-reduce.22
where the time goes:
time: 1030 us; the launch traced here: 1020 us
  waiting for transfers between devices  476 us (46%)
  matrix products  211 us (20%)
  blocking collectives  141 us (14%)
  local copies, waits for them, and re-layouts  91.2 us (9%)
  loops' own time  40.3 us (4%)
  other arithmetic  25.8 us (3%)
  starting transfers between devices  19.3 us (2%)
  between operations  17.2 us (2%)
    reduce_scatter x1, waiting for transfers between devices, local(): lax.psum_scatter(grad_upproj, ('blk', 'ulys'), scatter_dimension=0, tiled...  80.4 us
    reduce_scatter x1, waiting for transfers between devices, local(): lax.psum_scatter(grad_downproj, ('blk', 'ulys'), scatter_dimension=0, til...  80.3 us
    psum x1, waiting for transfers between devices, local(): lax.psum((shard_sums[0], shard_sums[1], shard_sums[2], shard_sums[3], sha...  52.7 us
    unnamed x2, blocking collectives  52.7 us
    all_gather x1, waiting for transfers between devices, local(): lax.all_gather(w_down, ('blk', 'ulys'), axis=0, tiled=True)  50.8 us
    reduce_scatter x1, waiting for transfers between devices, local(): lax.psum_scatter(grad_value, ('blk', 'ulys'), scatter_dimension=0, tiled=...  46.2 us
    reduce_scatter x1, waiting for transfers between devices, local(): lax.psum_scatter(grad_key, ('blk', 'ulys'), scatter_dimension=0, tiled=True)  45.7 us
    dot_general x6, matrix products, matmul_right_t(): lax.dot_general(left, right, (((1,), (1,)), ((), ())), precision=HIGH)  40.7 us
  transfers between devices with their start and end apart: 20, of which 15 were waited for; matrix products, arithmetic and copies ran while one was open for 18% of the time, Pallas kernels for 0%

commit v1 on v0

--- a/solution.py
+++ b/solution.py
@@ -242,7 +242,15 @@
     local_pairs = lax.psum_scatter(pair_grads, "blk", scatter_dimension=0, tiled=True)
     token_query_grad, token_keys_grad, token_values_grad = (
         lax.all_to_all(query_grad, "ulys", split_axis=0, concat_axis=1, tiled=True),
-        lax.all_to_all(local_pairs[:, :width], "ulys", split_axis=0, concat_axis=1, tiled=True),
+        jnp.concatenate(
+            lax.all_to_all(
+                jnp.stack(jnp.split(local_pairs[:, :width], lax.axis_size("ulys"), 0), 0),
+                axis_name="ulys",
+                split_axis=0,
+                concat_axis=0,
+            ),
+            1,
+        ),
         lax.all_to_all(local_pairs[:, width:], "ulys", split_axis=0, concat_axis=1, tiled=True),
     )
     grad_query = matmul_left_t(normalized_rows, token_query_grad)

time: 1030 us -> 1030 us (level)
    unnamed x152 -> x154, local copies, waits for them, and re-layouts: 38.2 us -> 39.1 us
where the time goes in v1:
time: 1030 us; the launch traced here: 1020 us
  waiting for transfers between devices  476 us (46%)
  matrix products  212 us (21%)
  blocking collectives  139 us (13%)
  local copies, waits for them, and re-layouts  91.3 us (9%)
  loops' own time  40.6 us (4%)
  other arithmetic  26.4 us (3%)
  starting transfers between devices  19.3 us (2%)
  between operations  17.2 us (2%)
    reduce_scatter x1, waiting for transfers between devices, local(): lax.psum_scatter(grad_upproj, ('blk', 'ulys'), scatter_dimension=0, tiled...  80.4 us
    reduce_scatter x1, waiting for transfers between devices, local(): lax.psum_scatter(grad_downproj, ('blk', 'ulys'), scatter_dimension=0, til...  80.3 us
    psum x1, waiting for transfers between devices, local(): lax.psum((shard_sums[0], shard_sums[1], shard_sums[2], shard_sums[3], sha...  53.8 us
    unnamed x2, blocking collectives  52.1 us
    all_gather x1, waiting for transfers between devices, local(): lax.all_gather(w_down, ('blk', 'ulys'), axis=0, tiled=True)  50.8 us
    reduce_scatter x1, waiting for transfers between devices, local(): lax.psum_scatter(grad_key, ('blk', 'ulys'), scatter_dimension=0, tiled=True)  46.3 us
    reduce_scatter x1, waiting for transfers between devices, local(): lax.psum_scatter(grad_value, ('blk', 'ulys'), scatter_dimension=0, tiled=...  45.7 us
    another operation x2, loops' own time, over_blocks(): state, unused = lax.scan(visit, state, (kv_blocks, code_blocks, offsets))  40.6 us
  transfers between devices with their start and end apart: 20, of which 15 were waited for; matrix products, arithmetic and copies ran while one was open for 18% of the time, Pallas kernels for 0%

profile of v1, /device:TPU:0, one launch (start us, length us, event | category | flops | bytes accessed | tf_op | source)
XLA Modules:
  0.0 1022.2 jit_solution(16879930637412951040)
XLA Ops:
  18.0 26.4 %all-reduce.18 = (f32[768]{0:T(1024)S(1)}, f32[768]{0:T(1024)S(1)}, f32[768]{0:T(1024)S(1)}, f32[768]{0:T(1024)}, f32[768]{0:T(1024)}, /*index=5*/f32[768]{0:T(1024)}, f32[768]{0:T(1024)}) all-reduce(f32[768]{0:T(1024)S(1)} %dynamic-update-slice.2, ...), channel_id=1, replica_groups=mesh['dp'=4,'blk'=2,'ulys'=4] {'blk','ulys'}, use_global_device_ids=true, to_apply=%add.2 | all-reduce | flops 5376 | bytes 43008
  55.1 19.6 %all-gather.10.cloned.1.call-done = f32[768,768]{1,0:T(8,128)} async-done(((f32[96,768]{1,0:T(8,128)}), f32[768,768]{1,0:T(8,128)}) %all-gather.10.cloned.1.call-update) | async-done | bytes 2359312 | tf_op jit(solution)/shard_map/all_gather | solution.py:80
  85.7 12.1 %all-to-all-done = f32[192,4,192]{0,2,1:T(8,128)S(1)} async-done(((f32[192,4,192]{0,2,1:T(8,128)}), f32[192,4,192]{0,2,1:T(8,128)S(1)}, u32[]{:S(2)}, u32[]{:S(2)}) %all-to-all-start) | async-done | bytes 589856 | tf_op jit(solution)/shard_map/all_to_all | solution.py:103
  129.3 16.9 %all-gather.14.cloned.1.call-done = f32[1536,384]{0,1:T(8,128)} async-done(((f32[768,384]{0,1:T(8,128)}), f32[1536,384]{0,1:T(8,128)}) %all-gather.14.cloned.1.call-update) | async-done | bytes 2359312 | tf_op jit(solution)/shard_map/all_gather | solution.py:167
  150.3 49.9 %while.28 = (s32[]{:T(128)}, f32[3,768]{1,0:T(4,128)S(1)}, f32[3,768]{1,0:T(4,128)}, f32[768,192]{0,1:T(8,128)S(1)}, f32[768]{0:T(1024)}, /*index=5*/f32[2,768]{...) while((s32[]{:T(128)}, f32[3,768]{1,0:T(4,128)S(1)}, ...), condition=%wide.region_5.6_spmd.clone, body=%wide.region_2.5_spmd.clone.sunk | while | flops 2741222400 | bytes 31506652 | solution.py:144
  205.9 22.2 %all-gather.1 = f32[8,1,384]{2,1,0:T(1,128)} all-gather(f32[1,1,384]{2,1,0:T(1,128)S(1)} %reshape.342), channel_id=1, replica_groups=mesh['dp'=4,'blk'=2,'ulys'=4] {'blk','ulys'}, dimensions={0}, use_global_device_ids=true | all-gather | bytes 13824 | tf_op jit(solution)/shard_map/all_gather | solution.py:86
  234.5 10.4 %all-gather.20.cloned.1.call-done = f32[768,3072]{1,0:T(8,128)} async-done(((f32[96,3072]{1,0:T(8,128)}), f32[768,3072]{1,0:T(8,128)}) %all-gather.20.cloned.1.call-update) | async-done | bytes 9437200 | tf_op jit(solution)/shard_map/all_gather | solution.py:85
  244.9 9.0 convolution_add_fusion
  253.9 50.8 %all-gather.22.cloned.1.call-done = f32[3072,768]{1,0:T(8,128)} async-done(((f32[384,768]{1,0:T(8,128)}), f32[3072,768]{1,0:T(8,128)}) %all-gather.22.cloned.1.call-update) | async-done | bytes 9437200 | tf_op jit(solution)/shard_map/all_gather | solution.py:87
  304.7 14.4 %fusion.64 = (f32[3072]{0:T(1024)}, f32[192,3072]{1,0:T(8,128)S(1)}) fusion(f32[192,3072]{1,0:T(8,128)S(1)} %convolution_add_fusion, f32[192,768]{1,0:T(8,128)} %param.28, f32[3072,768]{1,0:T(8,128)} %all-gather.22.cloned.1.call-done), kind=kOutput, calls=%fused_computation.128 | convolution fusion | flops 5449970688 | bytes 14757888 | tf_op jit(solution)/shard_map/dot_general | solution.py:36
  319.2 10.1 multiply_reduce_fusion
  340.4 11.0 %all-to-all-done.4 = f32[192,4,192]{2,0,1:T(8,128)} async-done(((f32[192,4,192]{2,0,1:T(8,128)}), f32[192,4,192]{2,0,1:T(8,128)}, u32[]{:S(2)}, u32[]{:S(2)}) %all-to-all-start.4) | async-done | bytes 589856 | tf_op jit(solution)/shard_map/all_to_all | solution.py:202
  357.7 124.2 %while.29 = (s32[]{:T(128)}, f32[768,192]{0,1:T(8,128)S(1)}, f32[1536,384]{0,1:T(8,128)}, f32[2,768,384]{1,2,0:T(8,128)}, f32[768]{0:T(1024)S(1)}, /*index=5*/f3...) while((s32[]{:T(128)}, f32[768,192]{0,1:T(8,128)S(1)}, ...), condition=%wide.region_12.13_spmd.clone, body=%wide.region_11.12_spmd.clone.sunk | while | flops 6813353472 | bytes 72011080 | solution.py:144
  390.5 8.8 fusion.164
  399.4 8.7 fusion.162
  439.0 8.8 fusion.164
  447.8 8.7 fusion.162
  487.1 14.1 %all_to_all.132 = f32[4,192,192]{2,1,0:T(8,128)S(1)} all-to-all(f32[4,192,192]{2,1,0:T(8,128)S(1)} %bitcast.220), channel_id=1, replica_groups=mesh['dp'=4,'blk'=2,'ulys'=4] {'ulys'}, dimensions={0} | all-to-all | bytes 1179648 | tf_op jit(solution)/shard_map/all_to_all | solution.py:244
  506.9 10.0 reduce-scatter.8.cloned.1.call-done
  518.4 14.2 %all_to_all.133 = f32[4,192,192]{1,2,0:T(8,128)S(1)} all-to-all(f32[4,192,192]{1,2,0:T(8,128)S(1)} %pad_maximum_fusion.1), channel_id=1, replica_groups=mesh['dp'=4,'blk'=2,'ulys'=4] {'ulys'}, dimensions={0} | all-to-all | bytes 1179648 | tf_op jit(solution)/shard_map/all_to_all | solution.py:246
  540.2 18.5 %all_to_all.134 = f32[4,192,192]{2,1,0:T(8,128)S(1)} all-to-all(f32[4,192,192]{2,1,0:T(8,128)S(1)} %bitcast.221), channel_id=1, replica_groups=mesh['dp'=4,'blk'=2,'ulys'=4] {'ulys'}, dimensions={0} | all-to-all | bytes 1179648 | tf_op jit(solution)/shard_map/all_to_all | solution.py:254
  566.4 11.0 %fusion.37 = f32[768,3072]{1,0:T(8,128)} fusion(f32[192,3072]{1,0:T(8,128)S(1)} %copy-done.14, f32[192,768]{1,0:T(8,128)S(1)} %copy-done.6, f32[768]{0:T(1024)S(1)} %copy-done.37, f32[768]{0:T(1024)S(1)} %copy-done.36, f32[192]{0:T(256)} %fusion.50, f32[192]{0:T(256)} %copy-done.41), kind=kOutput, calls=%fused_computation.83 | convolution fusion | flops 5436407808 | bytes 12393984 | tf_op jit(solution)/shard_map/dot_general | solution.py:32
  579.1 11.7 %fusion.36 = f32[3072,768]{1,0:T(8,128)} fusion(f32[192,768]{1,0:T(8,128)} %param.28, f32[192,3072]{1,0:T(8,128)S(1)} %copy-done.3), kind=kOutput, calls=%fused_computation.65 | convolution fusion | flops 5440536576 | bytes 12386304 | tf_op jit(solution)/shard_map/dot_general | solution.py:32
  590.9 23.7 %reduce-scatter.10.cloned.1.call-done = f32[96,768]{1,0:T(8,128)} async-done(((f32[768,768]{1,0:T(8,128)}), f32[96,768]{1,0:T(8,128)}) %reduce-scatter.10.cloned.1.call-update) | async-done | bytes 294928 | tf_op jit(solution)/shard_map/reduce_scatter | solution.py:271
  614.6 46.3 %reduce-scatter.12.cloned.1.call-done = f32[96,768]{1,0:T(8,128)} async-done(((f32[768,768]{1,0:T(8,128)}), f32[96,768]{1,0:T(8,128)}) %reduce-scatter.12.cloned.1.call-update) | async-done | bytes 294928 | tf_op jit(solution)/shard_map/reduce_scatter | solution.py:273
  660.8 45.7 %reduce-scatter.14.cloned.1.call-done = f32[96,768]{1,0:T(8,128)} async-done(((f32[768,768]{1,0:T(8,128)}), f32[96,768]{1,0:T(8,128)}) %reduce-scatter.14.cloned.1.call-update) | async-done | bytes 294928 | tf_op jit(solution)/shard_map/reduce_scatter | solution.py:274
  706.6 80.4 %reduce-scatter.18.cloned.1.call-done = f32[96,3072]{1,0:T(8,128)} async-done(((f32[768,3072]{1,0:T(8,128)}), f32[96,3072]{1,0:T(8,128)}) %reduce-scatter.18.cloned.1.call-update) | async-done | bytes 1179664 | tf_op jit(solution)/shard_map/reduce_scatter | solution.py:278
  787.0 80.3 %reduce-scatter.20.cloned.1.call-done = f32[384,768]{1,0:T(8,128)} async-done(((f32[3072,768]{1,0:T(8,128)}), f32[384,768]{1,0:T(8,128)}) %reduce-scatter.20.cloned.1.call-update) | async-done | bytes 1179664 | tf_op jit(solution)/shard_map/reduce_scatter | solution.py:280
  887.7 25.7 %all-reduce.17 = (f32[768]{0:T(1024)}, f32[768]{0:T(1024)}, f32[768]{0:T(1024)}, f32[768]{0:T(1024)}, f32[3072]{0:T(1024)}, /*index=5*/f32[768]{0:T(1024)}, f32[...) all-reduce(f32[768]{0:T(1024)} %dynamic-update-slice.7, ...), channel_id=1, replica_groups=mesh['dp'=4,'blk'=2,'ulys'=4] {'blk','ulys'}, use_global_device_ids=true, to_apply=%add.7 | all-reduce | flops 9984 | bytes 79872
  924.8 13.3 %all-reduce.19 = (f32[96]{0:T(128)}, f32[96]{0:T(128)}, f32[96]{0:T(128)}, f32[384]{0:T(512)}, f32[96]{0:T(128)}, /*index=5*/f32[96]{0:T(128)}, f32[96]{0:T(128)}, f32[96]{0:T(128)}, f32[96]{0:T(128)}) all-reduce(f32[96]{0:T(128)} %dynamic-slice.9, f32[96]{0:T(128)} %dynamic-slice.11, ...), channel_id=1, replica_groups=mesh['dp'=4,'blk'=2,'ulys'=4] {'dp'}, use_global_device_ids=true, to_apply=%region_20.21 | all-reduce | flops 1152 | bytes 9216 | tf_op jit(solution)/shard_map/psum | solution.py:287
  942.2 10.3 %fusion.35 = f32[192,768]{1,0:T(8,128)} fusion(f32[192,768]{1,0:T(8,128)S(1)} %copy-done.6, f32[3072,768]{1,0:T(8,128)} %all-gather.22.cloned.1.call-done, f32[192,3072]{1,0:T(8,128)S(1)} %copy-done.3, f32[768]{0:T(1024)S(1)} %copy-done.52), kind=kOutput, calls=%fused_computation.63 | convolution fusion | flops 5440831488 | bytes 12979200 | tf_op jit(solution)/shard_map/dot_general | solution.py:28
  952.5 53.8 %all-reduce.23.cloned.1.call-done = (f32[96,768]{1,0:T(8,128)}, f32[96,768]{1,0:T(8,128)}, f32[96,768]{1,0:T(8,128)}, f32[96,768]{1,0:T(8,128)}, f32[96,3072]{1,0:T(8,128)}, /*index=5*/f32[384,768]{1,0:T(8,128)}) async-done(((f32[96,768]{1,0:T(8,128)}, f32[96,768]{1,0:T(8,128)}, f32[96,768]{1,0:T(8,128)}, f32[96,768]{1,0:T(8,128)}, f32[96,3072]{1,0:T(8,128)}, /*index=5*/f32[384,768]{1,0:T(8,128)}), ...) | async-done | bytes 3538960 | tf_op jit(solution)/shard_map/psum | solution.py:287
  (336 shorter events, 267.5 us)
Async XLA Ops:
  7.2 39.7 %copy-start = (f32[192,768]{1,0:T(8,128)S(1)}, f32[192,768]{1,0:T(8,128)}, u32[]{:S(2)}) copy-start(f32[192,768]{1,0:T(8,128)} %param.24) | copy-start | bytes 1769476
  7.2 39.7 %all-gather.12.cloned.1.call-start = ((), (), s32[]{:S(2)}) async-start(), calls=%async_computation.16 | async-start | bytes 2654208 | tf_op jit(solution)/shard_map/all_gather | solution.py:81
  7.9 66.7 %all-gather.10.cloned.1.call-start = ((), (), s32[]{:S(2)}) async-start(), calls=%async_computation.15 | async-start | bytes 2654208 | tf_op jit(solution)/shard_map/all_gather | solution.py:80
  8.7 99.4 %all-gather.16.cloned.1.call-start = ((), (), s32[]{:S(2)}) async-start(), calls=%async_computation.18 | async-start | bytes 2654208 | tf_op jit(solution)/shard_map/all_gather | solution.py:78
  44.4 30.3 %copy-start.32 = (f32[768]{0:T(1024)}, f32[768]{0:T(1024)S(1)}, u32[]{:S(2)}) copy-start(f32[768]{0:T(1024)S(1)} %get-tuple-element.345) | copy-start | bytes 9220
  44.4 30.3 %copy-start.38 = (f32[768]{0:T(1024)}, f32[768]{0:T(1024)S(1)}, u32[]{:S(2)}) copy-start(f32[768]{0:T(1024)S(1)} %get-tuple-element.344) | copy-start | bytes 9220
  45.6 29.1 %copy-start.43 = (f32[192]{0:T(256)}, f32[192]{0:T(256)S(1)}, u32[]{:S(2)}) copy-start(f32[192]{0:T(256)S(1)} %broadcast_multiply_fusion.1) | copy-start | bytes 2308
  46.9 27.8 %copy-start.48 = (f32[192]{0:T(256)}, f32[192]{0:T(256)S(1)}, u32[]{:S(2)}) copy-start(f32[192]{0:T(256)S(1)} %fusion.49) | copy-start | bytes 2308
  51.6 29.5 %all-to-all-start.1 = ((f32[192,4,192]{0,2,1:T(8,128)}), f32[192,4,192]{0,2,1:T(8,128)S(1)}, u32[]{:S(2)}, u32[]{:S(2)}) async-start(f32[192,4,192]{0,2,1:T(8,128)} %bitcast.3), calls=%async_computation.1 | async-start | bytes 1572864 | tf_op jit(solution)/shard_map/all_to_all | solution.py:104
  81.1 16.7 %all-to-all-start = ((f32[192,4,192]{0,2,1:T(8,128)}), f32[192,4,192]{0,2,1:T(8,128)S(1)}, u32[]{:S(2)}, u32[]{:S(2)}) async-start(f32[192,4,192]{0,2,1:T(8,128)} %bitcast.1), calls=%async_computation | async-start | bytes 1572864 | tf_op jit(solution)/shard_map/all_to_all | solution.py:103
  84.6 61.6 %all-gather.14.cloned.1.call-start = ((), (), s32[]{:S(2)}) async-start(), calls=%async_computation.17 | async-start | bytes 3538944 | tf_op jit(solution)/shard_map/all_gather | solution.py:167
  99.9 129.2 %all-gather.18.cloned.1.call-start = ((), (), s32[]{:S(2)}) async-start(), calls=%async_computation.19 | async-start | bytes 2654208 | tf_op jit(solution)/shard_map/all_gather | solution.py:83
  100.5 144.3 %all-gather.20.cloned.1.call-start = ((), (), s32[]{:S(2)}) async-start(), calls=%async_computation.20 | async-start | bytes 10616832 | tf_op jit(solution)/shard_map/all_gather | solution.py:85
  101.1 203.6 %all-gather.22.cloned.1.call-start = ((), (), s32[]{:S(2)}) async-start(), calls=%async_computation.21 | async-start | bytes 10616832 | tf_op jit(solution)/shard_map/all_gather | solution.py:87
  113.2 15.2 %all-to-all-start.2 = ((f32[192,4,192]{2,0,1:T(8,128)}), f32[192,4,192]{2,0,1:T(8,128)S(1)}, u32[]{:S(2)}, u32[]{:S(2)}) async-start(f32[192,4,192]{2,0,1:T(8,128)} %copy.95), calls=%async_computation.2 | async-start | bytes 1572864 | tf_op jit(solution)/shard_map/all_to_all | solution.py:102
  200.2 27.9 %copy-start.20 = (f32[768,192]{0,1:T(8,128)}, f32[768,192]{0,1:T(8,128)S(1)}, u32[]{:S(2)}) copy-start(f32[768,192]{0,1:T(8,128)S(1)} %get-tuple-element.134) | copy-start | bytes 1769476
  202.2 27.0 %copy-start.57 = (f32[768]{0:T(1024)S(1)}, f32[768]{0:T(1024)}, u32[]{:S(2)}) copy-start(f32[768]{0:T(1024)} %get-tuple-element.347) | copy-start | bytes 9220
  202.2 25.9 %all-to-all-start.3 = ((f32[4,192,192]{2,1,0:T(8,128)}), f32[4,192,192]{2,1,0:T(8,128)S(1)}, u32[]{:S(2)}, u32[]{:S(2)}) async-start(f32[4,192,192]{2,1,0:T(8,128)} %bitcast.9), calls=%async_computation.3 | async-start | bytes 1572864 | tf_op jit(solution)/shard_map/all_to_all | solution.py:176
  253.9 65.2 %copy-start.2 = (f32[192,3072]{1,0:T(8,128)}, f32[192,3072]{1,0:T(8,128)S(1)}, u32[]{:S(2)}) copy-start(f32[192,3072]{1,0:T(8,128)S(1)} %convolution_add_fusion) | copy-start | bytes 7077892
  335.3 20.0 %copy-start.21 = (f32[768,192]{0,1:T(8,128)S(1)}, f32[768,192]{0,1:T(8,128)}, u32[]{:S(2)}) copy-start(f32[768,192]{0,1:T(8,128)} %copy-done.20) | copy-start | bytes 1769476
  335.3 16.1 %all-to-all-start.4 = ((f32[192,4,192]{2,0,1:T(8,128)}), f32[192,4,192]{2,0,1:T(8,128)}, u32[]{:S(2)}, u32[]{:S(2)}) async-start(f32[192,4,192]{2,0,1:T(8,128)} %copy.100), calls=%async_computation.4 | async-start | bytes 1572864 | tf_op jit(solution)/shard_map/all_to_all | solution.py:202
  339.7 177.2 %reduce-scatter.8.cloned.1.call-start = ((), (), s32[]{:S(2)}) async-start(), calls=%async_computation.22 | async-start | bytes 3538944 | tf_op jit(solution)/shard_map/reduce_scatter | solution.py:242
  482.0 108.9 %reduce-scatter.16.cloned.1.call-start = ((), (), s32[]{:S(2)}) async-start(), calls=%async_computation.26 | async-start | bytes 2654208 | tf_op jit(solution)/shard_map/reduce_scatter | solution.py:276
  486.8 127.8 %reduce-scatter.10.cloned.1.call-start = ((), (), s32[]{:S(2)}) async-start(), calls=%async_computation.23 | async-start | bytes 2654208 | tf_op jit(solution)/shard_map/reduce_scatter | solution.py:271
  487.1 16.0 %copy-start.34 = (f32[768]{0:T(1024)S(1)}, f32[768]{0:T(1024)}, u32[]{:S(2)}) copy-start(f32[768]{0:T(1024)} %copy-done.32) | copy-start | bytes 9220
  487.1 16.0 %copy-start.40 = (f32[768]{0:T(1024)S(1)}, f32[768]{0:T(1024)}, u32[]{:S(2)}) copy-start(f32[768]{0:T(1024)} %copy-done.38) | copy-start | bytes 9220
  506.8 154.0 %reduce-scatter.12.cloned.1.call-start = ((), (), s32[]{:S(2)}) async-start(), calls=%async_computation.24 | async-start | bytes 2654208 | tf_op jit(solution)/shard_map/reduce_scatter | solution.py:273
  538.9 167.7 %reduce-scatter.14.cloned.1.call-start = ((), (), s32[]{:S(2)}) async-start(), calls=%async_computation.25 | async-start | bytes 2654208 | tf_op jit(solution)/shard_map/reduce_scatter | solution.py:274
  566.3 220.7 %reduce-scatter.18.cloned.1.call-start = ((), (), s32[]{:S(2)}) async-start(), calls=%async_computation.27 | async-start | bytes 10616832 | tf_op jit(solution)/shard_map/reduce_scatter | solution.py:278
  577.4 289.8 %reduce-scatter.20.cloned.1.call-start = ((), (), s32[]{:S(2)}) async-start(), calls=%async_computation.28 | async-start | bytes 10616832 | tf_op jit(solution)/shard_map/reduce_scatter | solution.py:280
  590.8 278.4 %copy-start.61 = (f32[96]{0:T(128)S(1)}, f32[96]{0:T(128)}, u32[]{:S(2)}) copy-start(f32[96]{0:T(128)} %param.39) | copy-start | bytes 1156
  590.8 415.5 %all-reduce.23.cloned.1.call-start = ((), (), s32[]{:S(2)}) async-start(), calls=%async_computation.29 | async-start | bytes 7077888 | tf_op jit(solution)/shard_map/psum | solution.py:287
  (57 other events, 348.4 us)
Sparse Core Ops, SparseCore 0:
  9.9 32.0 all-gather.11
  43.9 30.6 all-gather.9
  76.5 31.5 all-gather.15
  110.1 36.0 all-gather.13
  147.9 29.0 all-gather.17
  178.8 66.0 all-gather.19
  246.8 57.9 all-gather.21
  482.1 34.7 reduce-scatter.7
  520.6 48.2 reduce-scatter.15
  572.1 42.4 reduce-scatter.9
  618.3 42.4 reduce-scatter.11
  664.0 42.4 reduce-scatter.13
  710.5 76.4 reduce-scatter.17
  790.7 76.4 reduce-scatter.19
  870.2 136.0 all-reduce.22
